TPU v7x, 32 devices: a whole 2x2x4 slice. The times are simulated.
32 devices in a mesh: ctx: 16 (over z, y, core), head: 2 (over x).
Axes of the slice: x: 2, y: 2, z: 4, core: 2. Of those that a mesh axis runs over, the one named last changes fastest.
Arguments:
- queries: bfloat16 [8192, 2048], P('ctx', 'head'), may hold values from -6 to 6
- keys: bfloat16 [8192, 2048], P('ctx', 'head'), may hold values from -6 to 6
- values: bfloat16 [8192, 2048], P('ctx', 'head'), may hold values from -6 to 6
- rates: float32 [8192, 2], P('ctx', 'head'), may hold values from 0.0005524272 to 0.0055242716
- w_up: bfloat16 [2, 1024, 512], P('head'), may hold values from -0.1875 to 0.1875
- w_gate: bfloat16 [2, 1024, 512], P('head'), may hold values from -0.1875 to 0.1875
- w_down: bfloat16 [2, 512, 1024], P('head'), may hold values from -0.25 to 0.25
- w_out: bfloat16 [2048, 5120], P('head'), may hold values from -0.125 to 0.125
Outputs:
- mixed: bfloat16 [8192, 5120], P('ctx', 'head')
All inputs are finite; a program needn't handle non-finite values.
Results may differ from a plain program's by a relative error of at most 0.018.
Values may be sent and summed in bfloat16 or wider, within the bound.
A program may use at most 128 MiB of HBM per device.

v0:
```python
import jax
import jax.numpy as jnp
from jax import lax
from jax.sharding import PartitionSpec as P

STEPS = 2


def frob(matrix):
    return jnp.sqrt(jnp.sum(matrix * matrix))


def tdot(left, right):
    return lax.dot_general(
        left, right, (((0,), (0,)), ((), ())), preferred_element_type=jnp.float32
    )


def local_grads(keys_h, targets, blocks):
    b_one, b_three, b_two = blocks
    act = jnp.dot(keys_h, b_one, preferred_element_type=jnp.float32)
    lin = jnp.dot(keys_h, b_three, preferred_element_type=jnp.float32)
    sig = jax.nn.sigmoid(act)
    hidden = (act * sig * lin).astype(jnp.bfloat16)
    err = jnp.dot(targets, b_two, preferred_element_type=jnp.float32)
    pgrad = (err * lin * sig * (1.0 + act * (1.0 - sig))).astype(jnp.bfloat16)
    qgrad = (err * act * sig).astype(jnp.bfloat16)
    return (tdot(keys_h, pgrad), tdot(keys_h, qgrad), tdot(targets, hidden))


def blocks_of(weights):
    return tuple((weight.astype(jnp.bfloat16) for weight in weights))


def shards(queries, keys, values, rates, w_up, w_gate, w_down, w_out):
    targets = (rates[:, 0][:, None] * values.astype(jnp.float32)).astype(jnp.bfloat16)
    weights = [
        w_up[0].astype(jnp.float32),
        w_gate[0].astype(jnp.float32),
        w_down[0].astype(jnp.float32).T,
    ]
    sizes = [frob(weights[0]), frob(weights[1]), frob(weights[2])]
    blocks = blocks_of(weights)
    for step in range(STEPS):
        grads = lax.psum(local_grads(keys, targets, blocks), "ctx")
        updated = []
        for weight, grad, size in zip(weights, grads, sizes):
            moved = weight + grad
            updated.append(moved * size / jnp.sqrt(jnp.sum(moved * moved) + 1e-06))
        weights = updated
        blocks = blocks_of(weights)
    b_one, b_three, b_two = blocks
    act = jnp.dot(queries, b_one, preferred_element_type=jnp.float32)
    lin = jnp.dot(queries, b_three, preferred_element_type=jnp.float32)
    hidq = (jax.nn.silu(act) * lin).astype(jnp.bfloat16)
    pieces = lax.dot_general(
        hidq, b_two, (((1,), (1,)), ((), ())), preferred_element_type=jnp.float32
    ).astype(jnp.bfloat16)
    partial_out = jnp.dot(pieces, w_out, preferred_element_type=jnp.float32)
    return lax.psum_scatter(
        partial_out.astype(jnp.bfloat16), "head", scatter_dimension=1, tiled=True
    )


def solution(mesh):
    return jax.shard_map(
        shards,
        mesh=mesh,
        in_specs=(
            P("ctx", "head"),
            P("ctx", "head"),
            P("ctx", "head"),
            P("ctx", "head"),
            P("head", None, None),
            P("head", None, None),
            P("head", None, None),
            P("head", None),
        ),
        out_specs=P("ctx", "head"),
        check_vma=False,
    )
```

profile of v0, /device:TPU:0, one launch (start us, length us, event | category | flops | bytes accessed | tf_op | source)
XLA Modules:
  0.0 430.4 jit_solution(6640502375833560063)
XLA Ops:
  6.5 1.2 copy-done
  7.8 1.9 fusion.5
  12.0 2.3 fusion.28
  14.3 2.4 convolution_bitcast_fusion.3
  16.7 2.2 convolution_bitcast_fusion.2
  19.0 1.1 copy-done.3
  20.1 1.3 copy.9
  22.0 1.5 copy.10
  23.5 137.7 %all-reduce.7.cloned.1.call-done = (f32[1024,512]{0,1:T(8,128)}, f32[1024,512]{0,1:T(8,128)}, f32[1024,512]{1,0:T(8,128)}) async-done(((f32[1024,512]{0,1:T(8,128)}, f32[1024,512]{0,1:T(8,128)}, f32[1024,512]{1,0:T(8,128)}), (f32[1024,512]{0,1:T(8,128)}, f32[1024,512]{0,1:T(8,128)}, f32[1024,512]{1,0:T(8,128)})) %all-reduce.7.cloned.1.call-update) | async-done | bytes 6291472 | tf_op jit(solution)/shard_map/psum | solution.py:45
  161.2 2.7 fusion.2
  165.2 4.1 fusion
  172.0 2.8 convolution_bitcast_fusion.6
  176.6 0.8 fusion.20
  177.4 2.2 convolution_bitcast_fusion
  179.6 2.4 convolution_bitcast_fusion.1
  182.0 2.3 fusion.29
  184.5 139.3 %all-reduce.5.cloned.1.call-done = (f32[1024,512]{1,0:T(8,128)}, f32[1024,512]{0,1:T(8,128)}, f32[1024,512]{0,1:T(8,128)}) async-done(((f32[1024,512]{1,0:T(8,128)}, f32[1024,512]{0,1:T(8,128)}, f32[1024,512]{0,1:T(8,128)}), (f32[1024,512]{1,0:T(8,128)}, f32[1024,512]{0,1:T(8,128)}, f32[1024,512]{0,1:T(8,128)})) %all-reduce.5.cloned.1.call-update) | async-done | bytes 6291472 | tf_op jit(solution)/shard_map/psum | solution.py:45
  323.9 3.7 multiply_reduce_fusion.2
  328.3 3.4 multiply_reduce_fusion.1
  332.3 3.4 multiply_reduce_fusion
  336.5 4.6 %convolution_bitcast_fusion.5 = f32[512,512]{1,0:T(8,128)} fusion(bf16[512,1024]{1,0:T(8,128)(2,1)} %param.8, f32[]{:T(128)S(6)} %sqrt.33, f32[]{:T(128)S(6)} %sqrt.27, f32[1024,512]{0,1:T(8,128)} %get-tuple-element.13, f32[1024,512]{0,1:T(8,128)} %get-tuple-element.15, bf16[1,1024,512]{1,2,0:T(8,128)(2,1)} %copy.9, f32[]{:T(128)S(6)} %sqrt.28), kind=kOutput, calls=%fused_computation.30 | convolution fusion | flops 541065216 | bytes 7340044 | tf_op jit(solution)/shard_map/dot_general | solution.py:53
  341.1 6.7 %convolution_convert_fusion.1 = bf16[512,1024]{1,0:T(8,128)(2,1)} fusion(bf16[512,1024]{1,0:T(8,128)(2,1)} %param.8, f32[]{:T(128)S(6)} %sqrt.35, f32[]{:T(128)S(6)} %sqrt.34, f32[512,512]{1,0:T(8,128)} %convolution_bitcast_fusion.5, f32[]{:T(128)S(6)} %sqrt.31, f32[]{:T(128)S(6)} %sqrt.29, f32[1024,512]{1,0:T(8,128)} %get-tuple-element.11, ...), kind=kOutput, calls=%fused_computation.27 | convolution fusion | flops 1084227584 | bytes 13631512 | tf_op jit(solution)/shard_map/dot_general | solution.py:56
  347.8 10.1 %convolution_convert_fusion = bf16[512,5120]{1,0:T(8,128)(2,1)} fusion(bf16[512,1024]{1,0:T(8,128)(2,1)} %convolution_convert_fusion.1, bf16[1024,5120]{1,0:T(8,128)(2,1)} %param.15), kind=kOutput, calls=%fused_computation | convolution fusion | flops 5371330560 | bytes 16777216 | tf_op jit(solution)/shard_map/dot_general | solution.py:59
  357.9 66.0 %reduce-scatter.2.cloned.1.call-done = bf16[512,2560]{1,0:T(8,128)(2,1)} async-done(((bf16[512,5120]{1,0:T(8,128)(2,1)}), bf16[512,2560]{1,0:T(8,128)(2,1)}) %reduce-scatter.2.cloned.1.call-update) | async-done | bytes 2621456 | tf_op jit(solution)/shard_map/reduce_scatter | solution.py:60
  (26 shorter events, 5.0 us)
Async XLA Ops:
  6.5 1.2 copy-start
  6.5 3.2 copy-start.4
  6.5 154.6 %all-reduce.7.cloned.1.call-start = ((), (), s32[]{:S(2)}) async-start(), calls=%async_computation.3 | async-start | bytes 12582912 | tf_op jit(solution)/shard_map/psum | solution.py:45
  9.7 1.2 copy-start.5
  9.7 1.5 copy-start.6
  9.7 1.5 copy-start.8
  18.9 1.2 copy-start.3
  18.9 305.0 %all-reduce.5.cloned.1.call-start = ((), (), s32[]{:S(2)}) async-start(), calls=%async_computation.2 | async-start | bytes 12582912 | tf_op jit(solution)/shard_map/psum | solution.py:45
  172.0 2.8 copy-start.1
  174.8 1.6 copy-start.2
  174.8 1.8 copy-start.7
  184.3 239.5 %reduce-scatter.2.cloned.1.call-start = ((), (), s32[]{:S(2)}) async-start(), calls=%async_computation.1 | async-start | bytes 7864320 | tf_op jit(solution)/shard_map/reduce_scatter | solution.py:60
Sparse Core Ops, SparseCore 0:
  19.0 142.1 all-reduce.6
  184.4 139.4 all-reduce.4
  358.0 65.8 reduce-scatter.1
where the time goes:
time: 431 us; the launch traced here: 430 us
  waiting for transfers between devices  343 us (80%)
  matrix products  42.9 us (10%)
  between operations  19.3 us (4%)
  other arithmetic  17.3 us (4%)
  local copies, waits for them, and re-layouts  7.57 us (2%)
    psum x2, waiting for transfers between devices, shards(): grads = lax.psum(local_grads(keys, targets, blocks), 'ctx')  277 us
    reduce_scatter x1, waiting for transfers between devices, shards(): lax.psum_scatter(partial_out.astype(jnp.bfloat16), 'head', scatter_dimens...  66 us
    dot_general x6, matrix products, tdot(): lax.dot_general(left, right, (((0,), (0,)), ((), ())), preferred_element_...  13.7 us
    reduce_sum x3, other arithmetic, shards(): updated.append(moved * size / jnp.sqrt(jnp.sum(moved * moved) + 1e-06))  10.5 us
    dot_general x1, matrix products, shards(): partial_out = jnp.dot(pieces, w_out, preferred_element_type=jnp.float32)  10.1 us
  transfers between devices with their start and end apart: 3, of which 3 were waited for; matrix products, arithmetic and copies ran while one was open for 1% of the time, Pallas kernels for 0%

commit v1 on v0

v1 whole, which is shorter than its diff:
```python
import jax
import jax.numpy as jnp
from jax import lax
from jax.sharding import PartitionSpec as P

STEPS = 2
F32 = jnp.float32
BF16 = jnp.bfloat16


def dot(left, right, dims=((1,), (0,))):
    return lax.dot_general(left, right, (dims, ((), ())), preferred_element_type=F32)


def shards(n_ctx, queries, keys, values, rates, w_up, w_gate, w_down, w_out):
    head = lax.axis_index("head")
    half = w_out.shape[1] // 2
    swap = [(0, 1), (1, 0)]
    w_near = lax.dynamic_slice_in_dim(w_out, head * half, half, 1)
    w_far = lax.ppermute(
        lax.dynamic_slice_in_dim(w_out, (1 - head) * half, half, 1), "head", swap
    )
    targets = (rates[:, 0][:, None] * values.astype(F32)).astype(BF16)
    blocks = jnp.stack([w_up[0], w_gate[0], w_down[0].T])
    sizes = jnp.sqrt(jnp.sum(blocks.astype(F32) ** 2, axis=(1, 2)))
    scales = jnp.ones((3,), F32)
    depth = blocks.shape[1] // n_ctx
    mine = lax.dynamic_slice_in_dim(
        blocks, lax.axis_index("ctx") * depth, depth, 1
    ).astype(F32)
    for step in range(STEPS):
        act = scales[0] * dot(keys, blocks[0])
        lin = scales[1] * dot(keys, blocks[1])
        err = scales[2] * dot(targets, blocks[2])
        sig = jax.nn.sigmoid(act)
        hidden = (act * sig * lin).astype(BF16)
        pgrad = (err * lin * sig * (1.0 + act * (1.0 - sig))).astype(BF16)
        qgrad = (err * act * sig).astype(BF16)
        rows = ((0,), (0,))
        grads = jnp.stack(
            [
                dot(keys, pgrad, rows).astype(BF16),
                dot(keys, qgrad, rows).astype(BF16),
                dot(targets, hidden, rows).astype(BF16),
            ]
        )
        total = lax.psum_scatter(grads, "ctx", scatter_dimension=1, tiled=True)
        moved = mine * scales[:, None, None] + total.astype(F32)
        mine = moved
        blocks = lax.all_gather(moved.astype(BF16), "ctx", axis=1, tiled=True)
        scales = sizes / jnp.sqrt(jnp.sum(blocks.astype(F32) ** 2, axis=(1, 2)) + 1e-06)
    act = scales[0] * dot(queries, blocks[0])
    lin = scales[1] * dot(queries, blocks[1])
    hidq = (jax.nn.silu(act) * lin).astype(BF16)
    near = (scales[2] * dot(hidq, blocks[2], ((1,), (1,)))).astype(BF16)
    far = lax.ppermute(near, "head", swap)
    return (dot(near, w_near) + dot(far, w_far)).astype(BF16)


def solution(mesh):
    def body(*args):
        return shards(mesh.shape["ctx"], *args)

    return jax.shard_map(
        body,
        mesh=mesh,
        in_specs=(
            P("ctx", "head"),
            P("ctx", "head"),
            P("ctx", "head"),
            P("ctx", "head"),
            P("head", None, None),
            P("head", None, None),
            P("head", None, None),
            P("head", None),
        ),
        out_specs=P("ctx", "head"),
        check_vma=False,
    )
```

time: 431 us -> 474 us (1.100)
  waiting for transfers between devices: 343 us -> 380 us
  local copies, waits for them, and re-layouts: 7.57 us -> 27 us
  matrix products: 42.9 us -> 31.7 us
  between operations: 19.3 us -> 14 us
    psum x2 -> x0, waiting for transfers between devices: 277 us -> none  [shards(): grads = lax.psum(local_grads(keys, targets, blocks), 'ctx')]
    unnamed x3 -> x6, waiting for transfers between devices: 0.05 us -> 217 us
    all_gather x0 -> x2, waiting for transfers between devices: none -> 82.7 us  [shards(): blocks = lax.all_gather(moved.astype(BF16), 'ctx', axis=1, tiled=True)]
    ppermute x0 -> x2, waiting for transfers between devices: none -> 80.3 us  [the longest x1 60.2 us: shards(): lax.ppermute(lax.dynamic_slice_in_dim(w_out, (1 - head) * half, half, 1),...]
    reduce_scatter x1 -> x0, waiting for transfers between devices: 66 us -> none  [shards(): lax.psum_scatter(partial_out.astype(jnp.bfloat16), 'head', scatter_dimens...]
    another operation x0 -> x2, local copies, waits for them, and re-layouts: none -> 15.2 us  [shards(): jnp.stack([dot(keys, pgrad, rows).astype(BF16), dot(keys, qgrad, rows).as...]
    dot_general x15 -> x16, matrix products: 42.9 us -> 31.7 us  [dot(): lax.dot_general(left, right, (dims, ((), ())), preferred_element_type=F32)]
    reduce_sum x5 -> x3, other arithmetic: 17.3 us -> 8.88 us  [the longest x2 5.63 us: shards(): jnp.sum(blocks.astype(F32) ** 2, axis=(1, 2)) + 1e-06]
  transfers between devices with their start and end apart: 3 -> 6, of which waited for: 3 -> 6; matrix products, arithmetic and copies ran while one was open for 1% -> 5% of each run, Pallas kernels for 0% -> 0%
where the time goes in v1:
time: 474 us; the launch traced here: 473 us
  waiting for transfers between devices  380 us (80%)
  matrix products  31.7 us (7%)
  local copies, waits for them, and re-layouts  27 us (6%)
  other arithmetic  16.4 us (3%)
  between operations  14 us (3%)
    unnamed x6, waiting for transfers between devices  217 us
    all_gather x2, waiting for transfers between devices, shards(): blocks = lax.all_gather(moved.astype(BF16), 'ctx', axis=1, tiled=True)  82.7 us
    ppermute x1, waiting for transfers between devices, shards(): lax.ppermute(lax.dynamic_slice_in_dim(w_out, (1 - head) * half, half, 1),...  60.2 us
    dot_general x16, matrix products, dot(): lax.dot_general(left, right, (dims, ((), ())), preferred_element_type=F32)  31.7 us
    ppermute x1, waiting for transfers between devices, shards(): far = lax.ppermute(near, 'head', swap)  20 us
    another operation x2, local copies, waits for them, and re-layouts, shards(): jnp.stack([dot(keys, pgrad, rows).astype(BF16), dot(keys, qgrad, rows).as...  15.2 us
  transfers between devices with their start and end apart: 6, of which 6 were waited for; matrix products, arithmetic and copies ran while one was open for 5% of the time, Pallas kernels for 0%

profile of v1, /device:TPU:0, one launch (start us, length us, event | category | flops | bytes accessed | tf_op | source)
XLA Modules:
  0.0 472.8 jit_solution(15701412564865319940)
XLA Ops:
  7.8 2.0 fusion.16
  14.2 2.0 pad_maximum_fusion.1
  16.2 7.6 %copy.30 = bf16[3,1024,512]{2,0,1:T(4,128)(2,1)} copy(bf16[3,1024,512]{1,2,0:T(8,128)(2,1)} %pad_maximum_fusion.1) | data formatting | bytes 6291456 | tf_op jit(solution)/shard_map/stack | solution.py:40
  23.9 1.5 copy.28
  26.7 3.3 multiply_reduce_fusion.2
  29.9 107.9 %all-reduce.5.cloned.1.call-done = bf16[3,1024,512]{2,0,1:T(4,128)(2,1)} async-done(((bf16[3,1024,512]{2,0,1:T(4,128)(2,1)}), bf16[3,1024,512]{2,0,1:T(4,128)(2,1)}) %all-reduce.5.cloned.1.call-update) | async-done | bytes 3145744
  138.9 1.7 fusion.33
  140.6 44.7 %all-gather.3.cloned.1.call-done = bf16[3,1024,512]{2,1,0:T(8,128)(2,1)} async-done(((bf16[3,64,512]{2,1,0:T(8,128)(2,1)}), bf16[3,1024,512]{2,1,0:T(8,128)(2,1)}) %all-gather.3.cloned.1.call-update) | async-done | bytes 3145744 | tf_op jit(solution)/shard_map/all_gather | solution.py:50
  185.3 2.9 multiply_reduce_fusion.1
  195.9 2.0 pad_maximum_fusion.2
  198.0 7.6 %copy.35 = bf16[3,1024,512]{2,0,1:T(4,128)(2,1)} copy(bf16[3,1024,512]{1,2,0:T(8,128)(2,1)} %pad_maximum_fusion.2) | data formatting | bytes 6291456 | tf_op jit(solution)/shard_map/stack | solution.py:40
  205.8 109.5 %all-reduce.7.cloned.1.call-done = bf16[3,1024,512]{2,0,1:T(4,128)(2,1)} async-done(((bf16[3,1024,512]{2,0,1:T(4,128)(2,1)}), bf16[3,1024,512]{2,0,1:T(4,128)(2,1)}) %all-reduce.7.cloned.1.call-update) | async-done | bytes 3145744
  316.3 1.8 add_convert_fusion.1
  318.1 5.1 %constant_dynamic-slice_fusion.2 = bf16[1024,2560]{1,0:T(8,128)(2,1)} fusion(bf16[1024,5120]{1,0:T(8,128)(2,1)} %param.15, s32[]{:T(128)S(6)} %select_n.11), kind=kLoop, calls=%fused_computation.72 | loop fusion | bytes 10485764 | tf_op jit(solution)/shard_map/dynamic_slice | solution.py:21
  323.2 1.5 collective-permute-start.1
  324.7 38.0 %all-gather.5.cloned.1.call-done = bf16[3,1024,512]{2,1,0:T(8,128)(2,1)} async-done(((bf16[3,64,512]{2,1,0:T(8,128)(2,1)}), bf16[3,1024,512]{2,1,0:T(8,128)(2,1)}) %all-gather.5.cloned.1.call-update) | async-done | bytes 3145744 | tf_op jit(solution)/shard_map/all_gather | solution.py:50
  362.7 2.7 multiply_reduce_fusion
  366.1 2.5 fusion.4
  368.6 4.2 multiply_convert_fusion
  372.9 1.5 collective-permute-start
  374.4 4.8 %fusion = f32[512,2560]{1,0:T(8,128)S(1)} fusion(bf16[512,1024]{1,0:T(8,128)(2,1)S(1)} %multiply_convert_fusion, bf16[1024,5120]{1,0:T(8,128)(2,1)} %param.15, s32[]{:T(128)S(6)} %select_n.10), kind=kOutput, calls=%fused_computation.4 | convolution fusion | flops 2684354560 | bytes 11534340 | tf_op jit(solution)/shard_map/dot_general | solution.py:12
  379.3 60.2 %collective-permute-done.1 = bf16[1024,2560]{1,0:T(8,128)(2,1)} collective-permute-done((bf16[1024,2560]{1,0:T(8,128)(2,1)}, bf16[1024,2560]{1,0:T(8,128)(2,1)}, u32[]{:S(2)}, u32[]{:S(2)}) %collective-permute-start.1) | collective-permute-done | bytes 5242912 | tf_op jit(solution)/shard_map/ppermute | solution.py:20
  439.5 20.0 %collective-permute-done = bf16[512,1024]{1,0:T(8,128)(2,1)S(1)} collective-permute-done((bf16[512,1024]{1,0:T(8,128)(2,1)S(1)}, bf16[512,1024]{1,0:T(8,128)(2,1)S(1)}, u32[]{:S(2)}, u32[]{:S(2)}) %collective-permute-start) | collective-permute-done | bytes 1048608 | tf_op jit(solution)/shard_map/ppermute | solution.py:56
  459.5 6.8 %add_convert_fusion = bf16[512,2560]{1,0:T(8,128)(2,1)} fusion(f32[512,2560]{1,0:T(8,128)S(1)} %fusion, bf16[512,1024]{1,0:T(8,128)(2,1)S(1)} %collective-permute-done, bf16[1024,2560]{1,0:T(8,128)(2,1)} %collective-permute-done.1), kind=kOutput, calls=%fused_computation.3 | convolution fusion | flops 2686976000 | bytes 14155776 | tf_op jit(solution)/shard_map/dot_general | solution.py:12
  (46 shorter events, 16.9 us)
Async XLA Ops:
  6.5 1.2 copy-start
  6.5 3.3 copy-start.3
  6.5 4.0 copy-start.4
  6.5 4.0 copy-start.8
  6.5 131.3 %all-reduce.5.cloned.1.call-start = ((), (), s32[]{:S(2)}) async-start(), calls=%async_computation.2 | async-start | bytes 8388608
  7.8 2.8 copy-start.5
  23.8 1.6 copy-start.9
  23.8 161.5 %all-gather.3.cloned.1.call-start = ((), (), s32[]{:S(2)}) async-start(), calls=%async_computation | async-start | bytes 3342336 | tf_op jit(solution)/shard_map/all_gather | solution.py:50
  140.6 174.7 %all-reduce.7.cloned.1.call-start = ((), (), s32[]{:S(2)}) async-start(), calls=%async_computation.3 | async-start | bytes 8388608
  185.3 3.5 copy-start.2
  188.9 2.8 copy-start.6
  205.6 157.1 %all-gather.5.cloned.1.call-start = ((), (), s32[]{:S(2)}) async-start(), calls=%async_computation.1 | async-start | bytes 3342336 | tf_op jit(solution)/shard_map/all_gather | solution.py:50
  323.2 42.9 %copy-start.7 = (bf16[512,1024]{1,0:T(8,128)(2,1)S(1)}, bf16[512,1024]{1,0:T(8,128)(2,1)}, u32[]{:S(2)}) copy-start(bf16[512,1024]{1,0:T(8,128)(2,1)} %param.8) | copy-start | bytes 3145732
  323.2 116.2 %collective-permute-start.1 = (bf16[1024,2560]{1,0:T(8,128)(2,1)}, bf16[1024,2560]{1,0:T(8,128)(2,1)}, u32[]{:S(2)}, u32[]{:S(2)}) collective-permute-start(bf16[1024,2560]{1,0:T(8,128)(2,1)} %constant_dynamic-slice_fusion.2), channel_id=1, source_target_pairs={{0,1},{1,0},{2,3},{3,2},{4,5},{5,4},{6,7},{7,6},{8,9},{9,8},{10,11... | collective-permute-start | bytes 15728648 | tf_op jit(solution)/shard_map/ppermute | solution.py:20
  372.9 86.6 %collective-permute-start = (bf16[512,1024]{1,0:T(8,128)(2,1)S(1)}, bf16[512,1024]{1,0:T(8,128)(2,1)S(1)}, u32[]{:S(2)}, u32[]{:S(2)}) collective-permute-start(bf16[512,1024]{1,0:T(8,128)(2,1)S(1)} %multiply_convert_fusion), channel_id=1, source_target_pairs={{0,1},{1,0},{2,3},{3,2},{4,5},{5,4},{6,7},{7,6},{8,9},{9,8},{10,11... | collective-permute-start | bytes 3145736 | tf_op jit(solution)/shard_map/ppermute | solution.py:56
  459.5 6.8 %copy-start.1 = (bf16[512,1024]{1,0:T(8,128)(2,1)S(1)}, bf16[512,1024]{1,0:T(8,128)(2,1)}, u32[]{:S(2)}) copy-start(bf16[512,1024]{1,0:T(8,128)(2,1)} %param.9) | copy-start | bytes 3145732
Sparse Core Ops, SparseCore 0:
  24.0 113.8 all-reduce.4
  140.7 44.6 all-gather.2
  205.7 109.5 all-reduce.6
  318.2 44.4 all-gather.4

commit v2 on v1

v2 whole, which is shorter than its diff:
```python
import functools

import jax
import jax.numpy as jnp
from jax import lax
from jax.experimental import pallas as pl
from jax.experimental.pallas import tpu as pltpu
from jax.sharding import PartitionSpec as P

STEPS = 2
F32 = jnp.float32
BF16 = jnp.bfloat16
MESH = pl.DeviceIdType.MESH
GROUP = 3


def orders_of(n_ctx):
    bits = list(range(n_ctx.bit_length() - 1))
    return [bits, bits[:1] + bits[2:] + bits[1:2]]


def bit_of(me, bit):
    return (me // (1 << bit)) % 2


def start_of(me, order, rows):
    start = 0
    for bit in order:
        rows = rows // 2
        start = start + bit_of(me, bit) * rows
    return start


def lanes_of(part, cols):
    width = cols // 2
    return slice(part * width, (part + 1) * width)


def exchange_kernel(n_ctx, g0, g1, g2, mine, o0, o1, o2, kept, sums, *scratch):
    grads, outs = (g0, g1, g2), (o0, o1, o2)
    rows, cols = g0.shape
    orders = orders_of(n_ctx)
    count = len(orders[0])
    recvs = scratch[:count]
    accs = scratch[count : 2 * count - 1]
    send_sem, recv_sem = scratch[2 * count - 1 :]
    me = lax.axis_index("ctx")

    def partner_of(bit):
        return me + (1 - 2 * bit_of(me, bit)) * (1 << bit)

    barrier = pltpu.get_barrier_semaphore()
    for bit in range(count):
        pl.semaphore_signal(
            barrier, inc=1, device_id={"ctx": partner_of(bit)}, device_id_type=MESH
        )
    pl.semaphore_wait(barrier, count)

    chains = [(w, part) for part in range(2) for w in range(GROUP)]
    copies = {}

    def send(chain, slot, source, target, bit):
        copy = pltpu.make_async_remote_copy(
            src_ref=source,
            dst_ref=target,
            send_sem=send_sem.at[chain, slot],
            recv_sem=recv_sem.at[chain, slot],
            device_id={"ctx": partner_of(bit)},
            device_id_type=MESH,
        )
        copy.start()
        copies[chain, slot] = copy

    def send_down(chain, stage):
        w, part = chains[chain]
        lanes = lanes_of(part, cols)
        bit = orders[part][stage]
        size = rows >> (stage + 1)
        away = pl.ds(pl.multiple_of((1 - bit_of(me, bit)) * size, size), size)
        if stage == 0:
            source = grads[w].at[away, lanes]
        else:
            source = accs[stage - 1].at[w, away, lanes]
        send(chain, stage, source, recvs[stage].at[w, :, lanes], bit)

    def region(chain, stage):
        w, part = chains[chain]
        size = rows >> stage
        start = start_of(me, orders[part][:stage], rows)
        return pl.ds(pl.multiple_of(start, size), size)

    def send_up(chain, stage):
        w, part = chains[chain]
        lanes = lanes_of(part, cols)
        place = outs[w].at[region(chain, stage + 1), lanes]
        send(chain, 2 * count - 1 - stage, place, place, orders[part][stage])

    def square_sum(block):
        return jnp.sum((block * block).reshape(-1, 8, block.shape[-1]), axis=0)

    for chain in range(len(chains)):
        send_down(chain, 0)
    for stage in range(count):
        size = rows >> (stage + 1)
        for chain, (w, part) in enumerate(chains):
            lanes = lanes_of(part, cols)
            bit = orders[part][stage]
            near = pl.ds(pl.multiple_of(bit_of(me, bit) * size, size), size)
            copies[chain, stage].wait_recv()
            held = grads[w][near, lanes] if stage == 0 else accs[stage - 1][w, near, lanes]
            total = held.astype(F32) + recvs[stage][w, :, lanes].astype(F32)
            if stage < count - 1:
                accs[stage][w, :, lanes] = total.astype(BF16)
                send_down(chain, stage + 1)
            else:
                moved = mine[part, w] + total
                kept[part, w] = moved
                rounded = moved.astype(BF16)
                outs[w][region(chain, count), lanes] = rounded
                send_up(chain, count - 1)
                sums[w, :, lanes] = square_sum(rounded.astype(F32))
    for stage in reversed(range(count)):
        size = rows >> (stage + 1)
        for chain, (w, part) in enumerate(chains):
            lanes = lanes_of(part, cols)
            copies[chain, 2 * count - 1 - stage].wait_recv()
            if stage > 0:
                send_up(chain, stage - 1)
            bit = orders[part][stage]
            other = start_of(me, orders[part][:stage], rows)
            other = other + (1 - bit_of(me, bit)) * size
            place = pl.ds(pl.multiple_of(other, size), size)
            sums[w, :, lanes] += square_sum(outs[w][place, lanes].astype(F32))
    for copy in copies.values():
        copy.wait_send()


def exchange(n_ctx, grads, mine):
    rows, cols = grads[0].shape
    count = n_ctx.bit_length() - 1
    full = jax.ShapeDtypeStruct((rows, cols), BF16)
    chains = 2 * GROUP
    sent = 2 * GROUP * rows * cols * 2
    return pl.pallas_call(
        functools.partial(exchange_kernel, n_ctx),
        out_shape=[
            full,
            full,
            full,
            jax.ShapeDtypeStruct(mine.shape, F32),
            jax.ShapeDtypeStruct((GROUP, 8, cols), F32),
        ],
        in_specs=[pl.BlockSpec(memory_space=pltpu.VMEM)] * 4,
        out_specs=[pl.BlockSpec(memory_space=pltpu.VMEM)] * 5,
        scratch_shapes=[
            pltpu.VMEM((GROUP, rows >> (stage + 1), cols), BF16)
            for stage in range(count)
        ]
        + [
            pltpu.VMEM((GROUP, rows >> (stage + 1), cols), BF16)
            for stage in range(count - 1)
        ]
        + [
            pltpu.SemaphoreType.DMA((chains, 2 * count)),
            pltpu.SemaphoreType.DMA((chains, 2 * count)),
        ],
        compiler_params=pltpu.CompilerParams(
            collective_id=0, has_side_effects=True, vmem_limit_bytes=32 << 20
        ),
        cost_estimate=pl.CostEstimate(
            flops=50_000_000, bytes_accessed=sent * 8, transcendentals=0
        ),
    )(*grads, mine)


def dot(left, right, dims=((1,), (0,))):
    return lax.dot_general(left, right, (dims, ((), ())), preferred_element_type=F32)


def shards(n_ctx, queries, keys, values, rates, w_up, w_gate, w_down, w_out):
    head = lax.axis_index("head")
    me = lax.axis_index("ctx")
    half = w_out.shape[1] // 2
    swap = [(0, 1), (1, 0)]
    w_near = lax.dynamic_slice_in_dim(w_out, head * half, half, 1)
    w_far = lax.ppermute(
        lax.dynamic_slice_in_dim(w_out, (1 - head) * half, half, 1), "head", swap
    )
    targets = (rates[:, 0][:, None] * values.astype(F32)).astype(BF16)
    blocks = [w_up[0], w_gate[0], w_down[0].T]
    rows, cols = blocks[0].shape
    sizes = jnp.stack([jnp.sqrt(jnp.sum(b.astype(F32) ** 2)) for b in blocks])
    scales = jnp.ones((GROUP,), F32)
    mine = jnp.stack(
        [
            jnp.stack(
                [
                    lax.dynamic_slice_in_dim(
                        b[:, lanes_of(part, cols)],
                        start_of(me, order, rows),
                        rows // n_ctx,
                        0,
                    )
                    for b in blocks
                ]
            )
            for part, order in enumerate(orders_of(n_ctx))
        ]
    ).astype(F32)
    for step in range(STEPS):
        act = scales[0] * dot(keys, blocks[0])
        lin = scales[1] * dot(keys, blocks[1])
        err = scales[2] * dot(targets, blocks[2])
        sig = jax.nn.sigmoid(act)
        hidden = (act * sig * lin).astype(BF16)
        pgrad = (err * lin * sig * (1.0 + act * (1.0 - sig))).astype(BF16)
        qgrad = (err * act * sig).astype(BF16)
        over = ((0,), (0,))
        grads = [
            dot(keys, pgrad, over).astype(BF16),
            dot(keys, qgrad, over).astype(BF16),
            dot(targets, hidden, over).astype(BF16),
        ]
        *blocks, mine, sums = exchange(n_ctx, grads, mine * scales[:, None, None])
        scales = sizes / jnp.sqrt(jnp.sum(sums, axis=(1, 2)) + 1e-06)
    act = scales[0] * dot(queries, blocks[0])
    lin = scales[1] * dot(queries, blocks[1])
    hidq = (jax.nn.silu(act) * lin).astype(BF16)
    near = (scales[2] * dot(hidq, blocks[2], ((1,), (1,)))).astype(BF16)
    far = lax.ppermute(near, "head", swap)
    return (dot(near, w_near) + dot(far, w_far)).astype(BF16)


def solution(mesh):
    def body(*args):
        return shards(mesh.shape["ctx"], *args)

    return jax.shard_map(
        body,
        mesh=mesh,
        in_specs=(
            P("ctx", "head"),
            P("ctx", "head"),
            P("ctx", "head"),
            P("ctx", "head"),
            P("head", None, None),
            P("head", None, None),
            P("head", None, None),
            P("head", None),
        ),
        out_specs=P("ctx", "head"),
        check_vma=False,
    )
```

time: 474 us -> 191 us (0.40)
  waiting for transfers between devices: 380 us -> 20.1 us
  Pallas kernels: 0 us -> 104 us
  between operations: 14 us -> 2.34 us
  other arithmetic: 16.4 us -> 4.77 us
  local copies, waits for them, and re-layouts: 27 us -> 16.5 us
  matrix products: 31.7 us -> 39.2 us
    unnamed x6 -> x0, waiting for transfers between devices: 217 us -> none
    pallas_call x0 -> x2, Pallas kernels: none -> 104 us  [exchange(): pl.pallas_call(functools.partial(exchange_kernel, n_ctx), out_shape=[full...]
    all_gather x2 -> x0, waiting for transfers between devices: 82.7 us -> none  [shards(): blocks = lax.all_gather(moved.astype(BF16), 'ctx', axis=1, tiled=True)]
    ppermute x1, waiting for transfers between devices: 60.2 us -> 0.01 us  [shards(): lax.ppermute(lax.dynamic_slice_in_dim(w_out, (1 - head) * half, half, 1),...]
    another operation x2, local copies, waits for them, and re-layouts: 15.2 us -> 0.03 us  [shards(): jnp.stack([lax.dynamic_slice_in_dim(b[:, lanes_of(part, cols)], start_of(...]
    dot_general x16, matrix products: 31.7 us -> 39.2 us  [dot(): lax.dot_general(left, right, (dims, ((), ())), preferred_element_type=F32)]
  transfers between devices with their start and end apart: 6 -> 2, of which waited for: 6 -> 1; matrix products, arithmetic and copies ran while one was open for 5% -> 22% of each run, Pallas kernels for 0% -> 55%
where the time goes in v2:
time: 191 us; the launch traced here: 190 us
  Pallas kernels  104 us (54%)
  matrix products  39.2 us (21%)
  waiting for transfers between devices  20.1 us (11%)
  local copies, waits for them, and re-layouts  16.5 us (9%)
  other arithmetic  4.77 us (2%)
  starting transfers between devices  3.51 us (2%)
  between operations  2.34 us (1%)
    pallas_call x2, Pallas kernels, exchange(): pl.pallas_call(functools.partial(exchange_kernel, n_ctx), out_shape=[full...  104 us
    dot_general x16, matrix products, dot(): lax.dot_general(left, right, (dims, ((), ())), preferred_element_type=F32)  39.2 us
    ppermute x1, waiting for transfers between devices, shards(): far = lax.ppermute(near, 'head', swap)  20.1 us
    unnamed x40, local copies, waits for them, and re-layouts  6.27 us
    dynamic_slice x1, local copies, waits for them, and re-layouts, shards(): lax.dynamic_slice_in_dim(w_out, (1 - head) * half, half, 1)  5.28 us
  transfers between devices with their start and end apart: 2, of which 1 were waited for; matrix products, arithmetic and copies ran while one was open for 22% of the time, Pallas kernels for 55%

profile of v2, /device:TPU:0, one launch (start us, length us, event | category | flops | bytes accessed | tf_op | source)
XLA Modules:
  0.0 190.2 jit_solution(6756408283555992536)
XLA Ops:
  0.0 5.3 %constant_dynamic-slice_fusion = bf16[1024,2560]{1,0:T(8,128)(2,1)} fusion(bf16[1024,5120]{1,0:T(8,128)(2,1)} %param.15, s32[]{:T(128)S(6)} %select_n.116), kind=kLoop, calls=%fused_computation.60 | loop fusion | bytes 10485764 | tf_op jit(solution)/shard_map/dynamic_slice | solution.py:187
  5.3 3.0 %collective-permute-start.1 = (bf16[1024,2560]{1,0:T(8,128)(2,1)}, bf16[1024,2560]{1,0:T(8,128)(2,1)}, u32[]{:S(2)}, u32[]{:S(2)}) collective-permute-start(bf16[1024,2560]{1,0:T(8,128)(2,1)} %constant_dynamic-slice_fusion), channel_id=1, source_target_pairs={{0,1},{1,0},{2,3},{3,2},{4,5},{5,4},{6,7},{7,6},{8,9},{9,8},{10,11... | collective-permute-start | bytes 15728648 | tf_op jit(solution)/shard_map/ppermute | solution.py:186
  8.3 1.2 multiply_reduce_fusion.1
  9.4 1.1 multiply_reduce_fusion.2
  10.6 1.7 fusion.30
  12.3 1.7 fusion.28
  14.0 1.2 multiply_reduce_fusion
  17.2 2.1 %fusion.12 = f32[512,512]{1,0:T(8,128)S(1)} fusion(bf16[1,512,1024]{2,1,0:T(8,128)(2,1)S(1)} %copy-done.8, bf16[512,1024]{1,0:T(8,128)(2,1)} %param.10, f32[512]{0:T(512)S(1)} %bitcast.84), kind=kOutput, calls=%fused_computation.29 | convolution fusion | flops 538443776 | bytes 3147776 | tf_op jit(solution)/shard_map/dot_general | solution.py:177
  19.3 2.9 %convolution_convert_fusion.3.g2 = bf16[1024,512]{1,0:T(8,128)(2,1)S(1)} fusion(f32[512,512]{1,0:T(8,128)S(1)} %copy-done.17, f32[512,512]{1,0:T(8,128)} %fusion.30, bf16[512,1024]{1,0:T(8,128)(2,1)} %param.10, f32[512]{0:T(512)S(1)} %bitcast.85), kind=kOutput, calls=%fused_computation.11 | convolution fusion | flops 540540928 | bytes 4196352 | tf_op jit(solution)/shard_map/dot_general | solution.py:177
  23.4 1.1 fusion.41
  25.7 1.4 fusion.40
  29.5 52.4 %shard_map.82 = (bf16[1024,512]{1,0:T(8,128)(2,1)S(1)}, bf16[1024,512]{1,0:T(8,128)(2,1)S(1)}, bf16[1024,512]{1,0:T(8,128)(2,1)S(1)}, f32[2,3,64,256]{3,2,1,0:T(8,128)S(1)}, f32[3,8,512]{2,1,0:T(8,128)S(1)}) custom-call(bf16[1024,512]{1,0:T(8,128)(2,1)S(1)} %fusion.7.g0, bf16[1024,512]{1,0:T(8,128)(2,1)S(1)} %fusion.8.g1, ...), custom_call_target="tpu_custom_call" | custom-call | flops 50000000 | bytes 50331648 | tf_op jit(solution)/shard_map/pallas_call | solution.py:144
  82.5 1.0 copy-done.2
  84.5 1.0 copy-done.6
  87.2 2.7 %fusion.6 = f32[512,512]{1,0:T(8,128)S(1)} fusion(bf16[512,1024]{1,0:T(8,128)(2,1)S(1)} %copy-done, bf16[1024,512]{1,0:T(8,128)(2,1)} %copy-done.6, f32[]{:T(128)} %bitcast.20), kind=kOutput, calls=%fused_computation.22 | convolution fusion | flops 537133056 | bytes 3145732 | tf_op jit(solution)/shard_map/dot_general | solution.py:177
  90.0 1.4 fusion.5
  91.5 1.4 convolution_multiply_fusion.4
  94.7 1.2 fusion.9.g0
  95.9 51.4 %shard_map.83 = (bf16[1024,512]{1,0:T(8,128)(2,1)S(1)}, bf16[1024,512]{1,0:T(8,128)(2,1)S(1)}, bf16[1024,512]{1,0:T(8,128)(2,1)S(1)}, f32[2,3,64,256]{3,2,1,0:T(8,128)}, f32[3,8,512]{2,1,0:T(8,128)S(1)}) custom-call(bf16[1024,512]{1,0:T(8,128)(2,1)S(1)} %fusion.9.g0, bf16[1024,512]{1,0:T(8,128)(2,1)S(1)} %fusion.10.g1, ...), custom_call_target="tpu_custom_call" | custom-call | flops 50000000 | bytes 50331648 | tf_op jit(solution)/shard_map/pallas_call | solution.py:144
  148.9 3.8 %fusion.4 = f32[512,512]{1,0:T(8,128)} fusion(bf16[512,1024]{1,0:T(8,128)(2,1)} %param.8, bf16[1024,512]{1,0:T(8,128)(2,1)} %copy-done.7, f32[]{:T(128)} %bitcast.27), kind=kOutput, calls=%fused_computation.18 | convolution fusion | flops 537133056 | bytes 3145732 | tf_op jit(solution)/shard_map/dot_general | solution.py:177
  152.8 5.0 %multiply_convert_fusion = bf16[512,1024]{1,0:T(8,128)(2,1)} fusion(bf16[1024,512]{1,0:T(8,128)(2,1)S(1)} %get-tuple-element.22, bf16[512,1024]{1,0:T(8,128)(2,1)} %param.8, bf16[1024,512]{1,0:T(8,128)(2,1)S(1)} %get-tuple-element.21, f32[512,512]{1,0:T(8,128)} %fusion.4, f32[]{:T(128)} %bitcast.26, f32[]{:T(128)} %bitcast.29), kind=kOutput, calls=%fused_computation.3 | convolution fusion | flops 1076625408 | bytes 5242888 | tf_op jit(solution)/shard_map/dot_general | solution.py:177
  158.3 5.1 %fusion = f32[512,2560]{1,0:T(8,128)S(1)} fusion(bf16[512,1024]{1,0:T(8,128)(2,1)} %multiply_convert_fusion, bf16[1024,5120]{1,0:T(8,128)(2,1)} %param.15, s32[]{:T(128)S(6)} %select_n.115), kind=kOutput, calls=%fused_computation.1 | convolution fusion | flops 2684354560 | bytes 11534340 | tf_op jit(solution)/shard_map/dot_general | solution.py:177
  163.4 20.1 %collective-permute-done = bf16[512,1024]{1,0:T(8,128)(2,1)S(1)} collective-permute-done((bf16[512,1024]{1,0:T(8,128)(2,1)}, bf16[512,1024]{1,0:T(8,128)(2,1)S(1)}, u32[]{:S(2)}, u32[]{:S(2)}) %collective-permute-start) | collective-permute-done | bytes 1048608 | tf_op jit(solution)/shard_map/ppermute | solution.py:230
  183.6 6.7 %add_convert_fusion = bf16[512,2560]{1,0:T(8,128)(2,1)} fusion(f32[512,2560]{1,0:T(8,128)S(1)} %fusion, bf16[512,1024]{1,0:T(8,128)(2,1)S(1)} %collective-permute-done, bf16[1024,2560]{1,0:T(8,128)(2,1)} %collective-permute-done.1), kind=kOutput, calls=%fused_computation | convolution fusion | flops 2686976000 | bytes 14155776 | tf_op jit(solution)/shard_map/dot_general | solution.py:177
  (60 shorter events, 12.2 us)
Async XLA Ops:
  0.0 10.6 %copy-start = (bf16[512,1024]{1,0:T(8,128)(2,1)S(1)}, bf16[512,1024]{1,0:T(8,128)(2,1)}, u32[]{:S(2)}) copy-start(bf16[512,1024]{1,0:T(8,128)(2,1)} %param.9) | copy-start | bytes 3145732
  0.0 8.3 %copy-start.10 = (bf16[1,1024,512]{2,1,0:T(8,128)(2,1)S(1)}, bf16[1,1024,512]{2,1,0:T(8,128)(2,1)}, u32[]{:S(2)}) copy-start(bf16[1,1024,512]{2,1,0:T(8,128)(2,1)} %param.13) | copy-start | bytes 3145732
  0.0 9.4 %copy-start.11 = (bf16[1,1024,512]{2,1,0:T(8,128)(2,1)S(1)}, bf16[1,1024,512]{2,1,0:T(8,128)(2,1)}, u32[]{:S(2)}) copy-start(bf16[1,1024,512]{2,1,0:T(8,128)(2,1)} %param.12) | copy-start | bytes 3145732
  5.3 178.3 %collective-permute-start.1 = (bf16[1024,2560]{1,0:T(8,128)(2,1)}, bf16[1024,2560]{1,0:T(8,128)(2,1)}, u32[]{:S(2)}, u32[]{:S(2)}) collective-permute-start(bf16[1024,2560]{1,0:T(8,128)(2,1)} %constant_dynamic-slice_fusion), channel_id=1, source_target_pairs={{0,1},{1,0},{2,3},{3,2},{4,5},{5,4},{6,7},{7,6},{8,9},{9,8},{10,11... | collective-permute-start | bytes 15728648 | tf_op jit(solution)/shard_map/ppermute | solution.py:186
  12.3 1.7 copy-start.8
  12.3 4.9 %copy-start.14 = (f32[512,1]{0,1:T(1,128)S(1)}, f32[512,1]{0,1:T(1,128)}, u32[]{:S(2)}) copy-start(f32[512,1]{0,1:T(1,128)} %param.11) | copy-start | bytes 6148
  17.2 2.1 %copy-start.17 = (f32[512,512]{1,0:T(8,128)S(1)}, f32[512,512]{1,0:T(8,128)}, u32[]{:S(2)}) copy-start(f32[512,512]{1,0:T(8,128)} %fusion.28) | copy-start | bytes 3145732
  19.3 2.9 %copy-start.18 = (f32[512,512]{1,0:T(8,128)}, f32[512,512]{1,0:T(8,128)S(1)}, u32[]{:S(2)}) copy-start(f32[512,512]{1,0:T(8,128)S(1)} %fusion.12) | copy-start | bytes 3145732
  19.3 2.9 %copy-start.15 = (f32[512,512]{1,0:T(8,128)S(1)}, f32[512,512]{1,0:T(8,128)}, u32[]{:S(2)}) copy-start(f32[512,512]{1,0:T(8,128)} %fusion.30) | copy-start | bytes 3145732
  22.2 1.2 copy-start.9
  25.7 1.5 copy-start.12
  27.0 1.3 copy-start.16
  27.0 1.6 copy-start.19
  81.9 0.6 copy-start.1
  82.5 1.0 copy-start.2
  83.5 1.0 copy-start.4
  84.5 1.0 copy-start.6
  87.1 2.8 %copy-start.5 = (bf16[1024,512]{1,0:T(8,128)(2,1)S(1)}, bf16[1024,512]{1,0:T(8,128)(2,1)}, u32[]{:S(2)}) copy-start(bf16[1024,512]{1,0:T(8,128)(2,1)} %copy-done.4) | copy-start | bytes 3145732
  89.9 1.5 copy-start.3
  89.9 1.5 copy-start.13
  147.2 1.0 copy-start.7
  157.8 25.8 %collective-permute-start = (bf16[512,1024]{1,0:T(8,128)(2,1)}, bf16[512,1024]{1,0:T(8,128)(2,1)S(1)}, u32[]{:S(2)}, u32[]{:S(2)}) collective-permute-start(bf16[512,1024]{1,0:T(8,128)(2,1)} %multiply_convert_fusion), channel_id=1, source_target_pairs={{0,1},{1,0},{2,3},{3,2},{4,5},{5,4},{6,7},{7,6},{8,9},{9,8},{10,11... | collective-permute-start | bytes 3145736 | tf_op jit(solution)/shard_map/ppermute | solution.py:230

commit v3 on v1

v3 whole, which is shorter than its diff:
```python
import functools

import jax
import jax.numpy as jnp
from jax import lax
from jax.experimental import pallas as pl
from jax.experimental.pallas import tpu as pltpu
from jax.sharding import PartitionSpec as P

STEPS = 2
F32 = jnp.float32
BF16 = jnp.bfloat16
MESH = pl.DeviceIdType.MESH
GROUP = 3


PARTS = 4


def orders_of(n_ctx):
    count = n_ctx.bit_length() - 1
    middle, low, high = list(range(1, count - 2)), count - 2, count - 1
    return [
        [0] + middle + [low, high],
        [0] + middle + [high, low],
        [0, low, high] + middle,
        [0, high, low] + middle,
    ]


def raw_bit(me, bit):
    return (me // (1 << bit)) % 2


def half_of(me, stage, count):
    if stage == count - 2:
        return (raw_bit(me, count - 2) + raw_bit(me, count - 1)) % 2
    return raw_bit(me, stage)


def partner_of(me, stage, count):
    flips = (count - 2, count - 1) if stage == count - 1 else (stage,)
    for bit in flips:
        me = me + (1 - 2 * raw_bit(me, bit)) * (1 << bit)
    return me


def lanes_of(part, cols):
    width = cols // PARTS
    return slice(part * width, (part + 1) * width)


def dot(left, right, dims=((1,), (0,))):
    return lax.dot_general(left, right, (dims, ((), ())), preferred_element_type=F32)


def square_sum(block):
    return jnp.sum((block * block).reshape(-1, 8, block.shape[-1]), axis=0)


def layer_kernel(
    n_ctx, q, k, v, r, w0, w1, w2, w_out, out, *scratch
):
    count = n_ctx.bit_length() - 1
    recvs, scratch = scratch[:count], scratch[count:]
    accs, scratch = scratch[: count - 1], scratch[count - 1 :]
    (
        kt, u, ut, first2, grads, blocks, mid, kept, sums,
        w_near, w_far, near, far, total_out,
        send_sem, recv_sem, swap_send, swap_recv, local_sem,
    ) = scratch
    tokens, rows = k.shape
    cols = w0.shape[1]
    half = w_out.shape[1] // 2
    orders = orders_of(n_ctx)
    me = lax.axis_index("ctx")
    head = lax.axis_index("head")

    def bit_of(stage):
        return half_of(me, stage, count)

    def partner(stage):
        return {"ctx": partner_of(me, stage, count)}

    def start_of(order):
        start, left = 0, rows
        for stage in order:
            left = left // 2
            start = start + bit_of(stage) * left
        return start

    across = {"head": 1 - head}
    barrier = pltpu.get_barrier_semaphore()
    for target in [partner(stage) for stage in range(count)] + [across]:
        pl.semaphore_signal(barrier, inc=1, device_id=target, device_id_type=MESH)
    pl.semaphore_wait(barrier, count + 1)

    def swap(slot, source, target):
        return pltpu.make_async_remote_copy(
            src_ref=source,
            dst_ref=target,
            send_sem=swap_send.at[slot],
            recv_sem=swap_recv.at[slot],
            device_id=across,
            device_id_type=MESH,
        )

    near_cols = pl.ds(pl.multiple_of(head * half, 128), half)
    far_cols = pl.ds(pl.multiple_of((1 - head) * half, 128), half)
    w_swap = swap(0, w_out.at[:, far_cols], w_far)
    w_swap.start()
    w_copy = pltpu.make_async_copy(w_out.at[:, near_cols], w_near, local_sem)
    w_copy.start()

    tile = tokens // 4
    for t in range(4):
        at = slice(t * tile, (t + 1) * tile)
        scaled = (r[at, :] * v[at, :].astype(F32)).astype(BF16)
        u[at, :] = scaled
        ut[:, at] = scaled.T
        kt[:, at] = k[at, :].T
    for t in range(cols // 128):
        at = slice(t * 128, (t + 1) * 128)
        first2[:, at] = w2[at, :].T

    chains = [(w, part) for w in range(GROUP) for part in range(PARTS)]
    firsts = (w0, w1, first2)
    scales = [None] * GROUP
    for step in range(STEPS):
        now = firsts if step == 0 else [blocks.at[w] for w in range(GROUP)]
        copies = {}

        def scaled_dot(w, left):
            product = dot(left, now[w][...])
            return product if scales[w] is None else product * scales[w]

        for t in range(2):
            at = slice(t * (tokens // 2), (t + 1) * (tokens // 2))
            act = scaled_dot(0, k[at, :])
            lin = scaled_dot(1, k[at, :])
            err = scaled_dot(2, u[at, :])
            sig = jax.nn.sigmoid(act)
            gate = act * sig
            mid[0, at, :] = (err * lin * sig * (1.0 + act * (1.0 - sig))).astype(BF16)
            mid[1, at, :] = (err * gate).astype(BF16)
            mid[2, at, :] = (gate * lin).astype(BF16)

        def send(chain, slot, source, target, bit):
            copy = pltpu.make_async_remote_copy(
                src_ref=source,
                dst_ref=target,
                send_sem=send_sem.at[chain, slot],
                recv_sem=recv_sem.at[chain, slot],
                device_id=partner(bit),
                device_id_type=MESH,
            )
            copy.start()
            copies[chain, slot] = copy

        def send_down(chain, stage):
            w, part = chains[chain]
            lanes = lanes_of(part, cols)
            bit = orders[part][stage]
            size = rows >> (stage + 1)
            away = pl.ds(pl.multiple_of((1 - bit_of(bit)) * size, size), size)
            origin = grads if stage == 0 else accs[stage - 1]
            source = origin.at[w, away, lanes]
            send(chain, stage, source, recvs[stage].at[w, :, lanes], bit)

        def region(chain, stage):
            w, part = chains[chain]
            size = rows >> stage
            start = start_of(orders[part][:stage])
            return pl.ds(pl.multiple_of(start, size), size)

        def send_up(chain, stage):
            w, part = chains[chain]
            place = blocks.at[w, region(chain, stage + 1), lanes_of(part, cols)]
            send(chain, 2 * count - 1 - stage, place, place, orders[part][stage])

        for w in range(GROUP):
            left = ut if w == 2 else kt

            def grad_rows(piece, carry):
                at = pl.ds(pl.multiple_of(piece * (rows // 4), rows // 4), rows // 4)
                grads[w, at, :] = dot(left[at, :], mid[w]).astype(BF16)
                return carry

            lax.fori_loop(0, 4, grad_rows, 0)
            for part in range(PARTS):
                send_down(PARTS * w + part, 0)
        if step == 0:
            norms = [
                jnp.sqrt(jnp.sum(square_sum(b[...].astype(F32)), keepdims=True))
                for b in firsts
            ]
        for stage in range(count):
            size = rows >> (stage + 1)
            for chain, (w, part) in enumerate(chains):
                lanes = lanes_of(part, cols)
                bit = orders[part][stage]
                close = pl.ds(pl.multiple_of(bit_of(bit) * size, size), size)
                copies[chain, stage].wait_recv()
                origin = grads if stage == 0 else accs[stage - 1]
                held = origin[w, close, lanes].astype(F32)
                total = held + recvs[stage][w, :, lanes].astype(F32)
                if stage < count - 1:
                    accs[stage][w, :, lanes] = total.astype(BF16)
                    send_down(chain, stage + 1)
                else:
                    place = region(chain, count)
                    if step == 0:
                        moved = firsts[w][place, lanes].astype(F32) + total
                    else:
                        moved = kept[w, :, lanes] * scales[w] + total
                    kept[w, :, lanes] = moved
                    rounded = moved.astype(BF16)
                    blocks[w, place, lanes] = rounded
                    send_up(chain, count - 1)
                    sums[w, :, lanes] = square_sum(rounded.astype(F32))
        for stage in reversed(range(count)):
            size = rows >> (stage + 1)
            for chain, (w, part) in enumerate(chains):
                lanes = lanes_of(part, cols)
                copies[chain, 2 * count - 1 - stage].wait_recv()
                if stage > 0:
                    send_up(chain, stage - 1)
                other = start_of(orders[part][:stage])
                other = other + (1 - bit_of(orders[part][stage])) * size
                place = pl.ds(pl.multiple_of(other, size), size)
                sums[w, :, lanes] += square_sum(blocks[w, place, lanes].astype(F32))
        for copy in copies.values():
            copy.wait_send()
        scales = [
            norms[w] / jnp.sqrt(jnp.sum(sums[w], keepdims=True) + 1e-06)
            for w in range(GROUP)
        ]

    o_swaps = []
    for t in range(4):
        at = slice(t * tile, (t + 1) * tile)
        act = dot(q[at, :], blocks[0]) * scales[0]
        lin = dot(q[at, :], blocks[1]) * scales[1]
        hidq = (act * jax.nn.sigmoid(act) * lin).astype(BF16)
        piece = dot(hidq, blocks[2], ((1,), (1,))) * scales[2]
        near[at, :] = piece.astype(BF16)
        o_swap = swap(1 + t, near.at[at, :], far.at[at, :])
        o_swap.start()
        o_swaps.append(o_swap)
    w_copy.wait()
    width = half // 5

    def near_cols_of(c, carry):
        lanes = pl.ds(pl.multiple_of(c * width, 128), width)
        total_out[:, lanes] = dot(near[...], w_near[:, lanes])
        return carry

    lax.fori_loop(0, 5, near_cols_of, 0)
    w_swap.wait()
    for t in range(4):
        at = slice(t * tile, (t + 1) * tile)
        o_swaps[t].wait_recv()

        def far_cols_of(c, carry):
            lanes = pl.ds(pl.multiple_of(c * width, 128), width)
            added = total_out[at, lanes] + dot(far[at, :], w_far[:, lanes])
            out[at, lanes] = added.astype(BF16)
            return carry

        lax.fori_loop(0, 5, far_cols_of, 0)
    for o_swap in o_swaps:
        o_swap.wait_send()


def shards(n_ctx, queries, keys, values, rates, w_up, w_gate, w_down, w_out):
    tokens, rows = keys.shape
    cols = w_up.shape[2]
    half = w_out.shape[1] // 2
    count = n_ctx.bit_length() - 1
    chains = PARTS * GROUP
    vmem = pl.BlockSpec(memory_space=pltpu.VMEM)
    return pl.pallas_call(
        functools.partial(layer_kernel, n_ctx),
        out_shape=jax.ShapeDtypeStruct((tokens, half), BF16),
        in_specs=[vmem] * 7 + [pl.BlockSpec(memory_space=pl.ANY)],
        out_specs=vmem,
        scratch_shapes=[
            pltpu.VMEM((GROUP, rows >> (stage + 1), cols), BF16)
            for stage in range(count)
        ]
        + [
            pltpu.VMEM((GROUP, rows >> (stage + 1), cols), BF16)
            for stage in range(count - 1)
        ]
        + [
            pltpu.VMEM((rows, tokens), BF16),
            pltpu.VMEM((tokens, rows), BF16),
            pltpu.VMEM((rows, tokens), BF16),
            pltpu.VMEM((rows, cols), BF16),
            pltpu.VMEM((GROUP, rows, cols), BF16),
            pltpu.VMEM((GROUP, rows, cols), BF16),
            pltpu.VMEM((GROUP, tokens, cols), BF16),
            pltpu.VMEM((GROUP, rows // n_ctx, cols), F32),
            pltpu.VMEM((GROUP, 8, cols), F32),
            pltpu.VMEM((rows, half), BF16),
            pltpu.VMEM((rows, half), BF16),
            pltpu.VMEM((tokens, rows), BF16),
            pltpu.VMEM((tokens, rows), BF16),
            pltpu.VMEM((tokens, half), F32),
            pltpu.SemaphoreType.DMA((chains, 2 * count)),
            pltpu.SemaphoreType.DMA((chains, 2 * count)),
            pltpu.SemaphoreType.DMA((5,)),
            pltpu.SemaphoreType.DMA((5,)),
            pltpu.SemaphoreType.DMA,
        ],
        compiler_params=pltpu.CompilerParams(
            collective_id=0, has_side_effects=True, vmem_limit_bytes=60 << 20
        ),
    )(queries, keys, values, rates, w_up[0], w_gate[0], w_down[0], w_out)


def solution(mesh):
    def body(*args):
        return shards(mesh.shape["ctx"], *args)

    return jax.shard_map(
        body,
        mesh=mesh,
        in_specs=(
            P("ctx", "head"),
            P("ctx", "head"),
            P("ctx", "head"),
            P("ctx", "head"),
            P("head", None, None),
            P("head", None, None),
            P("head", None, None),
            P("head", None),
        ),
        out_specs=P("ctx", "head"),
        check_vma=False,
    )
```

time: 474 us -> 155 us (0.33)
  waiting for transfers between devices: 380 us -> 0 us
  Pallas kernels: 0 us -> 150 us
  matrix products: 31.7 us -> 0 us
  local copies, waits for them, and re-layouts: 27 us -> 4.93 us
  other arithmetic: 16.4 us -> 0 us
  between operations: 14 us -> 0.01 us
    unnamed x6 -> x0, waiting for transfers between devices: 217 us -> none
    pallas_call x0 -> x1, Pallas kernels: none -> 150 us  [shards(): pl.pallas_call(functools.partial(layer_kernel, n_ctx), out_shape=jax.Shap...]
    all_gather x2 -> x0, waiting for transfers between devices: 82.7 us -> none  [shards(): blocks = lax.all_gather(moved.astype(BF16), 'ctx', axis=1, tiled=True)]
    ppermute x2 -> x0, waiting for transfers between devices: 80.3 us -> none  [the longest x1 60.2 us: shards(): lax.ppermute(lax.dynamic_slice_in_dim(w_out, (1 - head) * half, half, 1),...]
    dot_general x16 -> x0, matrix products: 31.7 us -> none  [dot(): lax.dot_general(left, right, (dims, ((), ())), preferred_element_type=F32)]
    another operation x2 -> x0, local copies, waits for them, and re-layouts: 15.2 us -> none  [shards(): jnp.stack([dot(keys, pgrad, rows).astype(BF16), dot(keys, qgrad, rows).as...]
    reduce_sum x3 -> x0, other arithmetic: 8.88 us -> none  [the longest x2 5.63 us: shards(): jnp.sum(blocks.astype(F32) ** 2, axis=(1, 2)) + 1e-06]
    dynamic_slice x1 -> x0, local copies, waits for them, and re-layouts: 5.13 us -> none  [shards(): lax.dynamic_slice_in_dim(w_out, (1 - head) * half, half, 1)]
  transfers between devices with their start and end apart: 6 -> 0, of which waited for: 6 -> 0; matrix products, arithmetic and copies ran while one was open for 5% -> 0% of each run, Pallas kernels for 0% -> 0%
where the time goes in v3:
time: 155 us
  Pallas kernels  150 us (97%)
  local copies, waits for them, and re-layouts  4.93 us (3%)
    pallas_call x1, Pallas kernels, shards(): pl.pallas_call(functools.partial(layer_kernel, n_ctx), out_shape=jax.Shap...  150 us
    unnamed x2, local copies, waits for them, and re-layouts  4.93 us

profile of v3, /device:TPU:0, one launch (start us, length us, event | category | flops | bytes accessed | tf_op | source)
XLA Modules:
  0.0 154.8 jit_solution(868388937015998205)
XLA Ops:
  0.0 1.5 copy.9.r
  1.5 149.8 %shard_map.82 = bf16[512,2560]{1,0:T(8,128)(2,1)} custom-call(bf16[512,1024]{1,0:T(8,128)(2,1)} %q.1, bf16[512,1024]{1,0:T(8,128)(2,1)} %k.1, bf16[512,1024]{1,0:T(8,128)(2,1)} %v.1, f32[512,1]{1,0:T(8,128)} %copy.9.r, bf16[1024,512]{1,0:T(8,128)(2,1)} %bitcast.3, bf16[1024,512]{1,0:T(8,128)(2,1)} %bitcast.4, bf16[512,1024]{1,0:T(8,128)(2,1)} %bitcast.5, ...), custom_call_target="tpu_custom_call" | custom-call | tf_op jit(solution)/shard_map/pallas_call | solution.py:282
  151.3 3.4 %copy.11 = bf16[512,2560]{1,0:T(8,128)(2,1)} copy(bf16[512,2560]{1,0:T(8,128)(2,1)} %shard_map.82) | data formatting | bytes 5242880

commit v4 on v3

--- a/solution.py
+++ b/solution.py
@@ -67,7 +67,7 @@
     (
         kt, u, ut, first2, grads, blocks, mid, kept, sums,
         w_near, w_far, near, far, total_out,
-        send_sem, recv_sem, swap_send, swap_recv, local_sem,
+        send_sem, recv_sem, swap_send, swap_recv, share_sem, local_sem,
     ) = scratch
     tokens, rows = k.shape
     cols = w0.shape[1]
@@ -107,7 +107,9 @@
 
     near_cols = pl.ds(pl.multiple_of(head * half, 128), half)
     far_cols = pl.ds(pl.multiple_of((1 - head) * half, 128), half)
-    w_swap = swap(0, w_out.at[:, far_cols], w_far)
+    depth = rows // 2
+    own_rows = pl.ds(pl.multiple_of(raw_bit(me, 0) * depth, depth), depth)
+    w_swap = swap(0, w_out.at[own_rows, far_cols], w_far.at[own_rows, :])
     w_swap.start()
     w_copy = pltpu.make_async_copy(w_out.at[:, near_cols], w_near, local_sem)
     w_copy.start()
@@ -236,6 +238,16 @@
             for w in range(GROUP)
         ]
 
+    w_swap.wait()
+    w_share = pltpu.make_async_remote_copy(
+        src_ref=w_far.at[own_rows, :],
+        dst_ref=w_far.at[own_rows, :],
+        send_sem=share_sem.at[0],
+        recv_sem=share_sem.at[1],
+        device_id=partner(0),
+        device_id_type=MESH,
+    )
+    w_share.start()
     o_swaps = []
     for t in range(4):
         at = slice(t * tile, (t + 1) * tile)
@@ -256,7 +268,7 @@
         return carry
 
     lax.fori_loop(0, 5, near_cols_of, 0)
-    w_swap.wait()
+    w_share.wait()
     for t in range(4):
         at = slice(t * tile, (t + 1) * tile)
         o_swaps[t].wait_recv()
@@ -311,6 +323,7 @@
             pltpu.SemaphoreType.DMA((chains, 2 * count)),
             pltpu.SemaphoreType.DMA((5,)),
             pltpu.SemaphoreType.DMA((5,)),
+            pltpu.SemaphoreType.DMA((2,)),
             pltpu.SemaphoreType.DMA,
         ],
         compiler_params=pltpu.CompilerParams(

time: 155 us -> 143 us (0.923)
  Pallas kernels: 150 us -> 138 us
    pallas_call x1, Pallas kernels: 150 us -> 138 us  [shards(): pl.pallas_call(functools.partial(layer_kernel, n_ctx), out_shape=jax.Shap...]
where the time goes in v4:
time: 143 us
  Pallas kernels  138 us (97%)
  local copies, waits for them, and re-layouts  4.93 us (3%)
    pallas_call x1, Pallas kernels, shards(): pl.pallas_call(functools.partial(layer_kernel, n_ctx), out_shape=jax.Shap...  138 us
    unnamed x2, local copies, waits for them, and re-layouts  4.93 us

profile of v4, /device:TPU:0, one launch (start us, length us, event | category | flops | bytes accessed | tf_op | source)
XLA Modules:
  0.0 143.2 jit_solution(14941814637520161725)
XLA Ops:
  0.0 1.5 %copy.9.r = f32[512,1]{1,0:T(8,128)} copy(f32[512,1]{0,1:T(1,128)} %param.11) | data formatting | bytes 4096 | tf_op args[3]
  1.5 138.2 %shard_map.82 = bf16[512,2560]{1,0:T(8,128)(2,1)} custom-call(bf16[512,1024]{1,0:T(8,128)(2,1)} %q.1, bf16[512,1024]{1,0:T(8,128)(2,1)} %k.1, bf16[512,1024]{1,0:T(8,128)(2,1)} %v.1, f32[512,1]{1,0:T(8,128)} %copy.9.r, bf16[1024,512]{1,0:T(8,128)(2,1)} %bitcast.3, bf16[1024,512]{1,0:T(8,128)(2,1)} %bitcast.4, bf16[512,1024]{1,0:T(8,128)(2,1)} %bitcast.5, ...), custom_call_target="tpu_custom_call" | custom-call | tf_op jit(solution)/shard_map/pallas_call | solution.py:294
  139.8 3.4 %copy.11 = bf16[512,2560]{1,0:T(8,128)(2,1)} copy(bf16[512,2560]{1,0:T(8,128)(2,1)} %shard_map.82) | data formatting | bytes 5242880

commit v5 on v4

--- a/solution.py
+++ b/solution.py
@@ -126,6 +126,9 @@
         first2[:, at] = w2[at, :].T
 
     chains = [(w, part) for w in range(GROUP) for part in range(PARTS)]
+    by_part = sorted(enumerate(chains), key=lambda item: item[1][1])
+    middle_first = by_part
+    ring_first = by_part[PARTS // 2 * GROUP :] + by_part[: PARTS // 2 * GROUP]
     firsts = (w0, w1, first2)
     scales = [None] * GROUP
     for step in range(STEPS):
@@ -198,7 +201,7 @@
             ]
         for stage in range(count):
             size = rows >> (stage + 1)
-            for chain, (w, part) in enumerate(chains):
+            for chain, (w, part) in ring_first if stage else list(enumerate(chains)):
                 lanes = lanes_of(part, cols)
                 bit = orders[part][stage]
                 close = pl.ds(pl.multiple_of(bit_of(bit) * size, size), size)
@@ -222,7 +225,7 @@
                     sums[w, :, lanes] = square_sum(rounded.astype(F32))
         for stage in reversed(range(count)):
             size = rows >> (stage + 1)
-            for chain, (w, part) in enumerate(chains):
+            for chain, (w, part) in middle_first if stage > 1 else ring_first:
                 lanes = lanes_of(part, cols)
                 copies[chain, 2 * count - 1 - stage].wait_recv()
                 if stage > 0:

time: 143 us -> 146 us (1.021)
  Pallas kernels: 138 us -> 141 us
    pallas_call x1, Pallas kernels: 138 us -> 141 us  [shards(): pl.pallas_call(functools.partial(layer_kernel, n_ctx), out_shape=jax.Shap...]
where the time goes in v5:
time: 146 us
  Pallas kernels  141 us (97%)
  local copies, waits for them, and re-layouts  4.93 us (3%)
    pallas_call x1, Pallas kernels, shards(): pl.pallas_call(functools.partial(layer_kernel, n_ctx), out_shape=jax.Shap...  141 us
    unnamed x2, local copies, waits for them, and re-layouts  4.93 us

profile of v5, /device:TPU:0, one launch (start us, length us, event | category | flops | bytes accessed | tf_op | source)
XLA Modules:
  0.0 146.3 jit_solution(3137620742335978488)
XLA Ops:
  0.0 1.5 %copy.9.r = f32[512,1]{1,0:T(8,128)} copy(f32[512,1]{0,1:T(1,128)} %param.11) | data formatting | bytes 4096 | tf_op args[3]
  1.5 141.3 %shard_map.82 = bf16[512,2560]{1,0:T(8,128)(2,1)} custom-call(bf16[512,1024]{1,0:T(8,128)(2,1)} %q.1, bf16[512,1024]{1,0:T(8,128)(2,1)} %k.1, bf16[512,1024]{1,0:T(8,128)(2,1)} %v.1, f32[512,1]{1,0:T(8,128)} %copy.9.r, bf16[1024,512]{1,0:T(8,128)(2,1)} %bitcast.3, bf16[1024,512]{1,0:T(8,128)(2,1)} %bitcast.4, bf16[512,1024]{1,0:T(8,128)(2,1)} %bitcast.5, ...), custom_call_target="tpu_custom_call" | custom-call | tf_op jit(solution)/shard_map/pallas_call | solution.py:297
  142.9 3.4 %copy.11 = bf16[512,2560]{1,0:T(8,128)(2,1)} copy(bf16[512,2560]{1,0:T(8,128)(2,1)} %shard_map.82) | data formatting | bytes 5242880
